TPU v7x, 256 devices: a whole 4x4x8 slice. The times are simulated.
256 devices in a mesh: blk: 32 (over x, z_lo, core), grp: 8 (over y, z_hi).
Axes of the slice: x: 4, y: 4, z: 8 (z_hi: 2, z_lo: 4; z = z_hi * 4 + z_lo), core: 2. Of those that a mesh axis runs over, the one named last changes fastest.
Arguments:
- activations: bfloat16 [16384, 8192], P('blk', 'grp'), may hold values from -6 to 6
- output_grads: bfloat16 [16384, 28672], P('blk', 'grp'), may hold values from -6 to 6
- query_left: bfloat16 [64, 32, 8192], P('blk', None, 'grp'), may hold values from -0.0078125 to 0.0078125
- query_right: bfloat16 [64, 32, 28672], P('blk', None, 'grp'), may hold values from -0.00390625 to 0.00390625
- basis_inputs: bfloat16 [32, 8192, 256], P('blk', 'grp'), may hold values from -0.0625 to 0.0625
- eigen_inputs: bfloat16 [32, 256], P('blk'), may hold values from 0.099609375 to 100
- basis_outputs: bfloat16 [32, 28672, 512], P('blk', 'grp'), may hold values from -0.03125 to 0.03125
- eigen_outputs: bfloat16 [32, 512], P('blk'), may hold values from 0.099609375 to 100
- owners: int32 [2], replicated, may hold values from 0 to 31
- seq_lengths: int32 [128], P('blk'), may hold values from 1 to 128, as said below
Outputs:
- scores: float32 [128, 64], P('blk')
Inputs may be any that keep to these rules, and one draw needn't show every extreme that they name: `seq_lengths`: the 4 lengths of one shard sum to at most 512; in every draw some shard is full (all its lengths 128) and some sequence has length 1.
All inputs are finite; a program needn't handle non-finite values.
Results may differ from a plain program's by a relative error of at most 0.02.
Values may be sent and summed in bfloat16 or wider, within the bound.
No kernel may reach another device: no remote copies, remote signals or barrier semaphores. Data moves between devices by JAX's collectives and lax.ppermute only.
A program may use at most 128 MiB of HBM per device.

v0:
```python
import jax
import jax.numpy as jnp
from jax import lax
from jax.sharding import PartitionSpec as P


def broadcast(x, axis, root):
    mine = lax.axis_index(axis) == root
    return lax.psum(jnp.where(mine, x, jnp.zeros_like(x)), axis)


def contract(row_block, factors):
    return lax.dot_general(
        row_block, factors, (((1,), (1,)), ((), ())), preferred_element_type=jnp.float32
    )


def finish(flat_rows, coeffs, basis, eigen):
    eigen_float = eigen.astype(jnp.float32)
    damped = (coeffs * (eigen_float / (1.0 + eigen_float))).astype(jnp.bfloat16)
    return (flat_rows.astype(jnp.float32) - contract(damped, basis)).astype(jnp.bfloat16)


def membership(seq_lens, slot_count):
    seq_ends = jnp.cumsum(seq_lens)
    seq_starts = seq_ends - seq_lens
    position = jnp.arange(slot_count, dtype=jnp.int32)[None, :]
    inside = (position >= seq_starts[:, None]) & (position < seq_ends[:, None])
    return inside.astype(jnp.float32)


def pair_scores(sum_left, sum_right, query_rank):
    product = (sum_left * sum_right).reshape(sum_left.shape[0], -1, query_rank)
    return jnp.sum(product, axis=2)


def local(
    activations,
    output_grads,
    query_left,
    query_right,
    basis_inputs,
    eigen_inputs,
    basis_outputs,
    eigen_outputs,
    owners,
    seq_lengths,
):
    basis_left, eigen_left = (
        broadcast(basis_inputs[0], "blk", owners[0]),
        broadcast(eigen_inputs[0], "blk", owners[0]),
    )
    basis_right, eigen_right = (
        broadcast(basis_outputs[0], "blk", owners[1]),
        broadcast(eigen_outputs[0], "blk", owners[1]),
    )
    query_rank = query_left.shape[1]
    left_flat = query_left.reshape(-1, query_left.shape[2])
    right_flat = query_right.reshape(-1, query_right.shape[2])
    left_coeffs = jnp.dot(left_flat, basis_left, preferred_element_type=jnp.float32)
    right_coeffs = jnp.dot(right_flat, basis_right, preferred_element_type=jnp.float32)
    left_coeffs, right_coeffs = (
        lax.psum(left_coeffs.astype(jnp.bfloat16), "grp").astype(jnp.float32),
        lax.psum(right_coeffs.astype(jnp.bfloat16), "grp").astype(jnp.float32),
    )
    left_ready = finish(left_flat, left_coeffs, basis_left, eigen_left).reshape(query_left.shape)
    right_ready = finish(right_flat, right_coeffs, basis_right, eigen_right).reshape(
        query_right.shape
    )
    slot_count = activations.shape[0]
    pieces = (
        lax.all_gather(left_ready, "blk", axis=0, tiled=True),
        lax.all_gather(right_ready, "blk", axis=0, tiled=True),
    )
    left_piece = pieces[0].reshape(-1, pieces[0].shape[2])
    right_piece = pieces[1].reshape(-1, pieces[1].shape[2])
    new_left = contract(activations, left_piece)
    new_right = contract(output_grads, right_piece)
    member = membership(seq_lengths, slot_count)
    sum_left, sum_right = (
        lax.psum(new_left.astype(jnp.bfloat16), "grp").astype(jnp.float32),
        lax.psum(new_right.astype(jnp.bfloat16), "grp").astype(jnp.float32),
    )
    result = jnp.dot(
        member,
        pair_scores(sum_left, sum_right, query_rank),
        precision=lax.Precision.HIGHEST,
        preferred_element_type=jnp.float32,
    )
    return result


def solution(mesh):
    in_specs = (
        P("blk", "grp"),
        P("blk", "grp"),
        P("blk", None, "grp"),
        P("blk", None, "grp"),
        P("blk", "grp", None),
        P("blk", None),
        P("blk", "grp", None),
        P("blk", None),
        P(),
        P("blk"),
    )
    out_specs = P("blk", None)
    return jax.shard_map(local, mesh=mesh, in_specs=in_specs, out_specs=out_specs, check_vma=False)
```

profile of v0, /device:TPU:1, one launch (start us, length us, event | category | flops | bytes accessed | tf_op | source)
XLA Modules:
  0.0 944.6 jit_solution(18013591543518392698)
XLA Ops:
  6.5 0.0 copy-start
  6.5 1.4 fusion.15
  9.2 0.0 copy-start.2
  9.2 2.1 select_bitcast_fusion
  11.3 0.9 select_bitcast_fusion.1
  12.2 0.0 all-reduce.9.cloned.1.call-update
  12.2 0.0 all-reduce.7.cloned.1.call-start
  12.3 0.0 copy-done.6
  12.4 70.3 %all-reduce = (bf16[512]{0:T(512)(128)(2,1)S(1)}, bf16[256]{0:T(256)(128)(2,1)S(1)}) all-reduce(bf16[512]{0:T(512)(128)(2,1)S(1)} %fusion.13, bf16[256]{0:T(256)(128)(2,1)S(1)} %fusion.14), channel_id=1, replica_groups=mesh['blk'=32,'grp'=8] {'blk'}, use_global_device_ids=true, to_apply=%region_7.8 | all-reduce | flops 768 | bytes 3072 | tf_op jit(solution)/shard_map/psum | solution.py:9
  82.7 227.5 %all-reduce.9.cloned.1.call-done = (bf16[3584,512]{1,0:T(8,128)(2,1)}, bf16[1024,256]{1,0:T(8,128)(2,1)}) async-done(((bf16[3584,512]{1,0:T(8,128)(2,1)}, bf16[1024,256]{1,0:T(8,128)(2,1)}), (bf16[3584,512]{1,0:T(8,128)(2,1)}, bf16[1024,256]{1,0:T(8,128)(2,1)})) %all-reduce.9.cloned.1.call-update) | async-done | bytes 4194320 | tf_op jit(solution)/shard_map/psum | solution.py:9
  310.2 3.9 fusion.4
  314.1 0.0 all-reduce.7.cloned.1.call-update
  314.2 0.0 all-gather.3.cloned.1.call-start
  314.2 0.3 fusion.5
  314.6 44.7 %psum.57 = bf16[64,256]{0,1:T(8,128)(2,1)S(1)} all-reduce(bf16[64,256]{0,1:T(8,128)(2,1)S(1)} %fusion.5), channel_id=1, replica_groups=mesh['blk'=32,'grp'=8] {'grp'}, use_global_device_ids=true, to_apply=%region_2.3 | all-reduce | flops 16384 | bytes 65536 | tf_op jit(solution)/shard_map/psum | solution.py:63
  359.3 1.0 fusion.3
  360.3 0.0 all-gather.3.cloned.1.call-update
  360.3 0.0 all-gather.5.cloned.1.call-start
  360.4 53.4 %all-reduce.7.cloned.1.call-done = bf16[64,512]{0,1:T(8,128)(2,1)} async-done(((bf16[64,512]{0,1:T(8,128)(2,1)}), bf16[64,512]{0,1:T(8,128)(2,1)}) %all-reduce.7.cloned.1.call-update) | async-done | bytes 65552 | tf_op jit(solution)/shard_map/psum | solution.py:64
  413.7 4.3 fusion
  418.0 0.0 all-gather.5.cloned.1.call-update
  418.0 0.0 all-reduce.11.cloned.1.call-start
  418.1 60.6 %all-gather.3.cloned.1.call-done = bf16[64,32,1024]{2,1,0:T(8,128)(2,1)} async-done(((bf16[2,32,1024]{2,1,0:T(8,128)(2,1)}), bf16[64,32,1024]{2,1,0:T(8,128)(2,1)}) %all-gather.3.cloned.1.call-update) | async-done | bytes 4194320 | tf_op jit(solution)/shard_map/all_gather | solution.py:72
  478.6 5.9 fusion.2
  484.5 83.8 %all-gather.5.cloned.1.call-done = bf16[64,32,3584]{2,1,0:T(8,128)(2,1)} async-done(((bf16[2,32,3584]{2,1,0:T(8,128)(2,1)}), bf16[64,32,3584]{2,1,0:T(8,128)(2,1)}) %all-gather.5.cloned.1.call-update) | async-done | bytes 14680080 | tf_op jit(solution)/shard_map/all_gather | solution.py:73
  568.3 13.1 %fusion.1 = bf16[512,2048]{0,1:T(8,128)(2,1)} fusion(bf16[2048,3584]{1,0:T(8,128)(2,1)} %bitcast.43, bf16[512,3584]{1,0:T(8,128)(2,1)} %param.11), kind=kOutput, calls=%fused_computation.7 | convolution fusion | flops 7517241344 | bytes 20447232 | tf_op jit(solution)/shard_map/dot_general | solution.py:13
  581.4 0.0 all-reduce.11.cloned.1.call-update
  581.4 0.6 copy-done.7
  582.1 0.2 reduce-window.8
  582.2 351.7 %all-reduce.11.cloned.1.call-done = (bf16[512,2048]{0,1:T(8,128)(2,1)}, bf16[512,2048]{0,1:T(8,128)(2,1)}) async-done(((bf16[512,2048]{0,1:T(8,128)(2,1)}, bf16[512,2048]{0,1:T(8,128)(2,1)}), (bf16[512,2048]{0,1:T(8,128)(2,1)}, bf16[512,2048]{0,1:T(8,128)(2,1)})) %all-reduce.11.cloned.1.call-update) | async-done | bytes 4194320 | tf_op jit(solution)/shard_map/psum | solution.py:82
  934.0 3.3 bitcast_reduce_fusion
  937.2 0.8 fusion.9
  (18 shorter events, 0.1 us)
Async XLA Ops:
  6.5 472.1 %copy-start = (bf16[512,1024]{1,0:T(8,128)(2,1)S(1)}, bf16[512,1024]{1,0:T(8,128)(2,1)}, u32[]{:S(2)}) copy-start(bf16[512,1024]{1,0:T(8,128)(2,1)} %param.10) | copy-start | bytes 3145732
  6.5 303.7 %all-reduce.9.cloned.1.call-start = ((), (), s32[]{:S(2)}) async-start(), calls=%async_computation.3 | async-start | bytes 8388608 | tf_op jit(solution)/shard_map/psum | solution.py:9
  9.2 2.1 copy-start.2
  11.3 1.0 copy-start.6
  11.3 1.0 copy-start.5
  11.3 298.9 %copy-start.4 = (bf16[2,32,3584]{2,1,0:T(8,128)(2,1)S(1)}, bf16[2,32,3584]{2,1,0:T(8,128)(2,1)}, u32[]{:S(2)}) copy-start(bf16[2,32,3584]{2,1,0:T(8,128)(2,1)} %param.13) | copy-start | bytes 1376260
  12.2 302.0 %copy-start.3 = (bf16[2,32,1024]{2,1,0:T(8,128)(2,1)S(1)}, bf16[2,32,1024]{2,1,0:T(8,128)(2,1)}, u32[]{:S(2)}) copy-start(bf16[2,32,1024]{2,1,0:T(8,128)(2,1)} %param.12) | copy-start | bytes 393220
  12.2 401.5 %all-reduce.7.cloned.1.call-start = ((), (), s32[]{:S(2)}) async-start(), calls=%async_computation.1 | async-start | bytes 262144 | tf_op jit(solution)/shard_map/psum | solution.py:64
  310.2 4.0 copy-start.1
  314.2 164.5 %all-gather.3.cloned.1.call-start = ((), (), s32[]{:S(2)}) async-start(), calls=%async_computation | async-start | bytes 4325376 | tf_op jit(solution)/shard_map/all_gather | solution.py:72
  360.3 208.0 %all-gather.5.cloned.1.call-start = ((), (), s32[]{:S(2)}) async-start(), calls=%async_computation.2 | async-start | bytes 15138816 | tf_op jit(solution)/shard_map/all_gather | solution.py:73
  418.0 515.9 %all-reduce.11.cloned.1.call-start = ((), (), s32[]{:S(2)}) async-start(), calls=%async_computation.4 | async-start | bytes 8388608 | tf_op jit(solution)/shard_map/psum | solution.py:82
  581.4 0.7 copy-start.7
Sparse Core Ops, SparseCore 0:
  12.4 297.7 all-reduce.8
  314.3 99.4 all-reduce.6
  415.6 62.9 all-gather.2
  480.3 87.9 all-gather.4
  581.5 352.3 all-reduce.10
where the time goes:
time: 945 us
  waiting for transfers between devices  777 us (82%)
  blocking collectives  115 us (12%)
  matrix products  29.3 us (3%)
  between operations  14.5 us (2%)
    psum x1, waiting for transfers between devices, local(): lax.psum(new_right.astype(jnp.bfloat16), 'grp').astype(jnp.float32)  352 us
    psum x1, waiting for transfers between devices, broadcast(): return lax.psum(jnp.where(mine, x, jnp.zeros_like(x)), axis)  228 us
    all_gather x1, waiting for transfers between devices, local(): lax.all_gather(right_ready, 'blk', axis=0, tiled=True)  83.8 us
    psum x1, blocking collectives, broadcast(): return lax.psum(jnp.where(mine, x, jnp.zeros_like(x)), axis)  70.3 us
    all_gather x1, waiting for transfers between devices, local(): lax.all_gather(left_ready, 'blk', axis=0, tiled=True)  60.6 us
    psum x1, waiting for transfers between devices, local(): lax.psum(right_coeffs.astype(jnp.bfloat16), 'grp').astype(jnp.float32)  53.4 us
    psum x1, blocking collectives, local(): lax.psum(left_coeffs.astype(jnp.bfloat16), 'grp').astype(jnp.float32)  44.7 us
    dot_general x4, matrix products, contract(): lax.dot_general(row_block, factors, (((1,), (1,)), ((), ())), preferred_e...  24.2 us
  transfers between devices with their start and end apart: 5, of which 5 were waited for; matrix products, arithmetic and copies ran while one was open for 1% of the time, Pallas kernels for 0%

commit v1 on v0

--- a/solution.py
+++ b/solution.py
@@ -79,7 +79,7 @@
     member = membership(seq_lengths, slot_count)
     sum_left, sum_right = (
         lax.psum(new_left.astype(jnp.bfloat16), "grp").astype(jnp.float32),
-        lax.psum(new_right.astype(jnp.bfloat16), "grp").astype(jnp.float32),
+        jnp.sum(lax.all_gather(new_right.astype(jnp.bfloat16), "grp"), axis=0).astype(jnp.float32),
     )
     result = jnp.dot(
         member,

time: 945 us -> 1090 us (1.15)
  waiting for transfers between devices: 777 us -> 901 us
  local copies, waits for them, and re-layouts: 2.06 us -> 13.6 us
    psum x1 -> x0, waiting for transfers between devices: 352 us -> none  [local(): lax.psum(new_right.astype(jnp.bfloat16), 'grp').astype(jnp.float32)]
    all_gather x0 -> x1, waiting for transfers between devices: none -> 323 us  [local(): lax.all_gather(new_right.astype(jnp.bfloat16), 'grp')]
    psum x1, waiting for transfers between devices: 53.4 us -> 203 us  [local(): lax.psum(right_coeffs.astype(jnp.bfloat16), 'grp').astype(jnp.float32)]
    reduce_sum x0 -> x1, other arithmetic: none -> 12.5 us  [local(): jnp.sum(lax.all_gather(new_right.astype(jnp.bfloat16), 'grp'), axis=0)]
    unnamed x16 -> x19, local copies, waits for them, and re-layouts: 0.66 us -> 12.2 us
  transfers between devices with their start and end apart: 5 -> 5, of which waited for: 5 -> 5; matrix products, arithmetic and copies ran while one was open for 1% -> 0% of each run, Pallas kernels for 0% -> 0%
where the time goes in v1:
time: 1090 us
  waiting for transfers between devices  901 us (83%)
  blocking collectives  115 us (11%)
  matrix products  31.5 us (3%)
  other arithmetic  16.7 us (2%)
  between operations  14.5 us (1%)
  local copies, waits for them, and re-layouts  13.6 us (1%)
    all_gather x1, waiting for transfers between devices, local(): lax.all_gather(new_right.astype(jnp.bfloat16), 'grp')  323 us
    psum x1, waiting for transfers between devices, broadcast(): return lax.psum(jnp.where(mine, x, jnp.zeros_like(x)), axis)  228 us
    psum x1, waiting for transfers between devices, local(): lax.psum(right_coeffs.astype(jnp.bfloat16), 'grp').astype(jnp.float32)  203 us
    all_gather x1, waiting for transfers between devices, local(): lax.all_gather(right_ready, 'blk', axis=0, tiled=True)  86.8 us
    psum x1, blocking collectives, broadcast(): return lax.psum(jnp.where(mine, x, jnp.zeros_like(x)), axis)  70.3 us
    all_gather x1, waiting for transfers between devices, local(): lax.all_gather(left_ready, 'blk', axis=0, tiled=True)  60 us
    psum x1, blocking collectives, local(): lax.psum(left_coeffs.astype(jnp.bfloat16), 'grp').astype(jnp.float32)  44.7 us
    dot_general x4, matrix products, contract(): lax.dot_general(row_block, factors, (((1,), (1,)), ((), ())), preferred_e...  25.4 us
  transfers between devices with their start and end apart: 5, of which 5 were waited for; matrix products, arithmetic and copies ran while one was open for 0% of the time, Pallas kernels for 0%

profile of v1, /device:TPU:1, one launch (start us, length us, event | category | flops | bytes accessed | tf_op | source)
XLA Modules:
  0.0 1092.1 jit_solution(7021698275654287336)
XLA Ops:
  6.5 1.4 fusion.15
  9.2 0.0 copy-start.3
  9.2 2.0 select_bitcast_fusion
  11.3 0.9 select_bitcast_fusion.1
  12.1 0.0 all-reduce.6.cloned.1.call-update
  12.2 0.0 all-gather.5.cloned.1.call-start
  12.3 70.3 %all-reduce = (bf16[512]{0:T(512)(128)(2,1)S(1)}, bf16[256]{0:T(256)(128)(2,1)S(1)}) all-reduce(bf16[512]{0:T(512)(128)(2,1)S(1)} %fusion.13, bf16[256]{0:T(256)(128)(2,1)S(1)} %fusion.14), channel_id=1, replica_groups=mesh['blk'=32,'grp'=8] {'blk'}, use_global_device_ids=true, to_apply=%region_7.8 | all-reduce | flops 768 | bytes 3072 | tf_op jit(solution)/shard_map/psum | solution.py:9
  82.6 227.5 %all-reduce.6.cloned.1.call-done = (bf16[3584,512]{1,0:T(8,128)(2,1)}, bf16[1024,256]{1,0:T(8,128)(2,1)}) async-done(((bf16[3584,512]{1,0:T(8,128)(2,1)}, bf16[1024,256]{1,0:T(8,128)(2,1)}), (bf16[3584,512]{1,0:T(8,128)(2,1)}, bf16[1024,256]{1,0:T(8,128)(2,1)})) %all-reduce.6.cloned.1.call-update) | async-done | bytes 4194320 | tf_op jit(solution)/shard_map/psum | solution.py:9
  310.1 1.4 fusion.5
  311.5 44.7 %psum.50 = bf16[64,256]{0,1:T(8,128)(2,1)S(1)} all-reduce(bf16[64,256]{0,1:T(8,128)(2,1)S(1)} %fusion.5), channel_id=1, replica_groups=mesh['blk'=32,'grp'=8] {'grp'}, use_global_device_ids=true, to_apply=%region_2.3 | all-reduce | flops 16384 | bytes 65536 | tf_op jit(solution)/shard_map/psum | solution.py:63
  356.2 2.1 fusion.3
  358.3 0.0 all-gather.5.cloned.1.call-update
  358.3 0.0 all-reduce.8.cloned.1.call-start
  358.3 3.9 fusion.4
  362.2 60.0 %all-gather.5.cloned.1.call-done = bf16[64,32,1024]{2,1,0:T(8,128)(2,1)} async-done(((bf16[2,32,1024]{2,1,0:T(8,128)(2,1)}), bf16[64,32,1024]{2,1,0:T(8,128)(2,1)}) %all-gather.5.cloned.1.call-update) | async-done | bytes 4194320 | tf_op jit(solution)/shard_map/all_gather | solution.py:72
  422.2 6.0 fusion.2
  428.2 0.0 all-reduce.8.cloned.1.call-update
  428.2 0.0 all-gather.7.cloned.1.call-start
  428.3 202.7 %all-reduce.8.cloned.1.call-done = (bf16[64,512]{0,1:T(8,128)(2,1)}, bf16[512,2048]{0,1:T(8,128)(2,1)}) async-done(((bf16[64,512]{0,1:T(8,128)(2,1)}, bf16[512,2048]{0,1:T(8,128)(2,1)}), (bf16[64,512]{0,1:T(8,128)(2,1)}, bf16[512,2048]{0,1:T(8,128)(2,1)})) %all-reduce.8.cloned.1.call-update) | async-done | bytes 2162704 | tf_op jit(solution)/shard_map/psum | solution.py:64
  631.0 4.3 fusion
  635.2 0.0 all-gather.7.cloned.1.call-update
  635.3 0.2 all-gather.9.cloned.1.call-start
  635.5 86.8 %all-gather.7.cloned.1.call-done = bf16[64,32,3584]{2,1,0:T(8,128)(2,1)} async-done(((bf16[2,32,3584]{2,1,0:T(8,128)(2,1)}), bf16[64,32,3584]{2,1,0:T(8,128)(2,1)}) %all-gather.7.cloned.1.call-update) | async-done | bytes 14680080 | tf_op jit(solution)/shard_map/all_gather | solution.py:73
  722.3 13.1 %fusion.1 = bf16[512,2048]{0,1:T(8,128)(2,1)} fusion(bf16[2048,3584]{1,0:T(8,128)(2,1)} %bitcast.49, bf16[512,3584]{1,0:T(8,128)(2,1)} %param.11), kind=kOutput, calls=%fused_computation.8 | convolution fusion | flops 7517241344 | bytes 20447232 | tf_op jit(solution)/shard_map/dot_general | solution.py:13
  735.3 0.0 all-gather.9.cloned.1.call-update
  735.4 0.2 reduce-window.8
  735.6 323.5 %all-gather.9.cloned.1.call-done = bf16[4096,2048]{0,1:T(8,128)(2,1)} async-done(((bf16[512,2048]{0,1:T(8,128)(2,1)}), bf16[4096,2048]{0,1:T(8,128)(2,1)}) %all-gather.9.cloned.1.call-update) | async-done | bytes 16777232 | tf_op jit(solution)/shard_map/all_gather | solution.py:82
  1059.0 12.1 %copy.11 = bf16[256,8,8,512]{3,2,1,0:T(8,128)(2,1)S(1)} copy(bf16[256,8,8,512]{3,1,2,0:T(8,128)(2,1)} %bitcast.41) | data formatting | bytes 33554432
  1071.2 0.0 copy-start.1
  1071.2 12.5 %bitcast_reduce_fusion = bf16[512,2048]{0,1:T(8,128)(2,1)S(1)} fusion(bf16[256,8,8,512]{3,2,1,0:T(8,128)(2,1)S(1)} %copy.11), kind=kLoop, calls=%fused_computation | loop fusion | flops 7340032 | bytes 18874368 | tf_op jit(solution)/shard_map/reduce_sum | solution.py:82
  1083.7 1.0 bitcast_reduce_fusion.1
  1084.8 0.8 fusion.9
  (22 shorter events, 0.1 us)
Async XLA Ops:
  6.5 415.7 %copy-start = (bf16[512,1024]{1,0:T(8,128)(2,1)S(1)}, bf16[512,1024]{1,0:T(8,128)(2,1)}, u32[]{:S(2)}) copy-start(bf16[512,1024]{1,0:T(8,128)(2,1)} %param.10) | copy-start | bytes 3145732
  6.5 303.6 %all-reduce.6.cloned.1.call-start = ((), (), s32[]{:S(2)}) async-start(), calls=%async_computation.3 | async-start | bytes 8388608 | tf_op jit(solution)/shard_map/psum | solution.py:9
  9.2 2.1 copy-start.3
  11.2 1.0 copy-start.7
  11.2 1.0 copy-start.6
  11.2 298.9 %copy-start.4 = (bf16[2,32,1024]{2,1,0:T(8,128)(2,1)S(1)}, bf16[2,32,1024]{2,1,0:T(8,128)(2,1)}, u32[]{:S(2)}) copy-start(bf16[2,32,1024]{2,1,0:T(8,128)(2,1)} %param.12) | copy-start | bytes 393220
  11.2 347.1 %copy-start.5 = (bf16[2,32,3584]{2,1,0:T(8,128)(2,1)S(1)}, bf16[2,32,3584]{2,1,0:T(8,128)(2,1)}, u32[]{:S(2)}) copy-start(bf16[2,32,3584]{2,1,0:T(8,128)(2,1)} %param.13) | copy-start | bytes 1376260
  12.2 410.0 %all-gather.5.cloned.1.call-start = ((), (), s32[]{:S(2)}) async-start(), calls=%async_computation | async-start | bytes 4325376 | tf_op jit(solution)/shard_map/all_gather | solution.py:72
  358.3 272.7 %all-reduce.8.cloned.1.call-start = ((), (), s32[]{:S(2)}) async-start(), calls=%async_computation.4 | async-start | bytes 4456448 | tf_op jit(solution)/shard_map/psum | solution.py:64
  428.2 294.1 %all-gather.7.cloned.1.call-start = ((), (), s32[]{:S(2)}) async-start(), calls=%async_computation.1 | async-start | bytes 15138816 | tf_op jit(solution)/shard_map/all_gather | solution.py:73
  635.3 423.8 %all-gather.9.cloned.1.call-start = ((), (), s32[]{:S(2)}) async-start(), calls=%async_computation.2 | async-start | bytes 18874368 | tf_op jit(solution)/shard_map/all_gather | solution.py:82
  722.3 13.1 %copy-start.8 = (s32[4]{0:T(128)S(1)}, s32[4]{0:T(128)}, u32[]{:S(2)}) copy-start(s32[4]{0:T(128)} %param.19) | copy-start | bytes 52
  1071.2 12.5 %copy-start.2 = (bf16[512,2048]{0,1:T(8,128)(2,1)S(1)}, bf16[512,2048]{0,1:T(8,128)(2,1)}, u32[]{:S(2)}) copy-start(bf16[512,2048]{0,1:T(8,128)(2,1)} %get-tuple-element.10) | copy-start | bytes 6291460
  1071.2 14.4 %copy-start.1 = (bf16[512,1024]{1,0:T(8,128)(2,1)S(1)}, bf16[512,1024]{1,0:T(8,128)(2,1)}, u32[]{:S(2)}) copy-start(bf16[512,1024]{1,0:T(8,128)(2,1)} %param.10) | copy-start | bytes 3145732
Sparse Core Ops, SparseCore 0:
  12.3 297.7 all-reduce.5
  358.4 63.7 all-gather.4
  428.3 202.5 all-reduce.7
  635.4 86.8 all-gather.6
  735.5 323.5 all-gather.8
